TPU v7x, 32 devices: a whole 2x2x4 slice. The times are simulated.
32 devices in a mesh: dp: 16 (over z, y, core), mp: 2 (over x).
Axes of the slice: x: 2, y: 2, z: 4, core: 2. Of those that a mesh axis runs over, the one named last changes fastest.
Arguments:
- hidden_in: bfloat16 [32768, 1024], P(('dp', 'mp')), may hold values from -6 to 6
- out_grad: bfloat16 [32768, 1024], P(('dp', 'mp')), may hold values from -6 to 6
- ln1_gain: float32 [1024], replicated, may hold values from 0.5 to 1.5
- ln1_bias: float32 [1024], replicated, may hold values from -3 to 3
- w_query: bfloat16 [1024, 1024], P(None, 'mp'), may hold values from -0.1875 to 0.1875
- w_key: bfloat16 [1024, 1024], P(None, 'mp'), may hold values from -0.1875 to 0.1875
- w_value: bfloat16 [1024, 1024], P(None, 'mp'), may hold values from -0.1875 to 0.1875
- w_out: bfloat16 [1024, 1024], P('mp'), may hold values from -1.5 to 1.5
- ln2_gain: float32 [1024], replicated, may hold values from 0.5 to 1.5
- ln2_bias: float32 [1024], replicated, may hold values from -3 to 3
- w_up: bfloat16 [1024, 4096], P(None, 'mp'), may hold values from -0.1875 to 0.1875
- b_up: float32 [4096], P('mp'), may hold values from -3 to 3
- w_down: bfloat16 [4096, 1024], P('mp'), may hold values from -0.09375 to 0.09375
- b_down: float32 [1024], replicated, may hold values from -3 to 3
- rand_blocks: int32 [16, 16, 3], P('mp'), may hold values from 0 to 15
Outputs:
- output: bfloat16 [32768, 1024], P(('dp', 'mp'))
- input_grad: float32 [32768, 1024], P(('dp', 'mp'))
- grad_ln1_gain: float32 [1024], replicated
- grad_ln1_bias: float32 [1024], replicated
- grad_w_query: float32 [1024, 1024], P(None, 'mp')
- grad_w_key: float32 [1024, 1024], P(None, 'mp')
- grad_w_value: float32 [1024, 1024], P(None, 'mp')
- grad_w_out: float32 [1024, 1024], P('mp')
- grad_ln2_gain: float32 [1024], replicated
- grad_ln2_bias: float32 [1024], replicated
- grad_w_up: float32 [1024, 4096], P(None, 'mp')
- grad_b_up: float32 [4096], P('mp')
- grad_w_down: float32 [4096, 1024], P('mp')
- grad_b_down: float32 [1024], replicated
Inputs may be any that keep to these rules, and one draw needn't show every extreme that they name: rand_blocks[h, i, r] is a key block of the same sequence; entries may repeat or fall on window or global blocks, and those of the first and last query blocks have no effect.
All inputs are finite; a program needn't handle non-finite values.
Results may differ from a plain program's by a relative error of at most 0.02.
Values may be sent and summed in bfloat16 or wider, within the bound.
A program may use at most 320 MiB of HBM per device.

v0:
```python
import jax
import jax.numpy as jnp
from jax import lax
from jax.sharding import PartitionSpec as P

HD = 64
BLOCK = 64
SEQ = 1024


def layer_norm(values, norm_gain, norm_bias):
    center = values - jnp.mean(values, axis=-1, keepdims=True)
    spread = jnp.mean(center * center, axis=-1, keepdims=True)
    return center * lax.rsqrt(spread + 1e-05) * norm_gain + norm_bias


def block_mask(rand_blocks):
    blocks = SEQ // BLOCK
    row_ids = jnp.arange(blocks)[:, None]
    col_ids = jnp.arange(blocks)[None, :]
    window = (
        (jnp.abs(row_ids - col_ids) <= 1)
        | (col_ids == 0)
        | (col_ids == blocks - 1)
        | (row_ids == 0)
        | (row_ids == blocks - 1)
    )
    picked = jnp.any(rand_blocks[:, :, :, None] == jnp.arange(blocks)[None, None, None, :], axis=2)
    allowed = window[None] | picked
    return jnp.repeat(jnp.repeat(allowed, BLOCK, axis=1), BLOCK, axis=2)


def attend_forward(joined_seq, allowed, scaling):
    queries = joined_seq[:, 0]
    key_rows = joined_seq[:, 1]
    value_rows = joined_seq[:, 2]
    scores = (
        jnp.einsum("qhd,khd->hqk", queries, key_rows, preferred_element_type=jnp.float32) * scaling
    )
    scores = jnp.where(allowed, scores, -1e30)
    highest = jnp.max(scores, axis=-1, keepdims=True)
    shifted = jnp.exp(scores - highest)
    row_totals = jnp.sum(shifted, axis=-1, keepdims=True)
    attn_probs = (shifted / row_totals).astype(jnp.bfloat16)
    context = jnp.einsum("hqk,khd->qhd", attn_probs, value_rows, preferred_element_type=jnp.float32)
    return (context.astype(jnp.bfloat16), (highest + jnp.log(row_totals))[..., 0])


def attend_backward(seq_items, allowed, scaling):
    joined_seq, grad_context, row_lse = seq_items
    queries = joined_seq[:, 0]
    key_rows = joined_seq[:, 1]
    value_rows = joined_seq[:, 2]
    scores = (
        jnp.einsum("qhd,khd->hqk", queries, key_rows, preferred_element_type=jnp.float32) * scaling
    )
    scores = jnp.where(allowed, scores, -1e30)
    attn_probs = jnp.exp(scores - row_lse[..., None])
    grad_values = jnp.einsum(
        "hqk,qhd->khd",
        attn_probs.astype(jnp.bfloat16),
        grad_context,
        preferred_element_type=jnp.float32,
    ).astype(jnp.bfloat16)
    grad_probs = jnp.einsum(
        "qhd,khd->hqk", grad_context, value_rows, preferred_element_type=jnp.float32
    )
    row_inner = jnp.sum(grad_probs * attn_probs, axis=-1, keepdims=True)
    grad_scores = (attn_probs * (grad_probs - row_inner)).astype(jnp.bfloat16)
    grad_queries = (
        jnp.einsum("hqk,khd->qhd", grad_scores, key_rows, preferred_element_type=jnp.float32)
        * scaling
    ).astype(jnp.bfloat16)
    grad_keys = (
        jnp.einsum("hqk,qhd->khd", grad_scores, queries, preferred_element_type=jnp.float32)
        * scaling
    ).astype(jnp.bfloat16)
    return jnp.stack([grad_queries, grad_keys, grad_values], axis=1)


def per_device(
    hidden_in,
    out_grad,
    ln1_gain,
    ln1_bias,
    w_query,
    w_key,
    w_value,
    w_out,
    ln2_gain,
    ln2_bias,
    w_up,
    b_up,
    w_down,
    b_down,
    rand_blocks,
):
    local_heads = rand_blocks.shape[0]
    head_width = local_heads * HD
    local_rows = hidden_in.shape[0]
    seq_count = local_rows * lax.axis_size("mp") // SEQ
    scaling = HD ** (-0.5)
    allowed = block_mask(rand_blocks)
    inputs = hidden_in.astype(jnp.float32)
    w_joined = jnp.concatenate([w_query, w_key, w_value], axis=1)
    normed_one = layer_norm(inputs, ln1_gain, ln1_bias).astype(jnp.bfloat16)
    rows_one = lax.all_gather(normed_one, "mp", axis=0, tiled=True)
    joined = jnp.dot(rows_one, w_joined, preferred_element_type=jnp.float32).astype(jnp.bfloat16)
    joined_seq = joined.reshape(seq_count, SEQ, 3, local_heads, HD)
    context, row_lse = lax.map(
        lambda seq_block: attend_forward(seq_block, allowed, scaling), joined_seq
    )
    context_rows = context.reshape(seq_count * SEQ, head_width)
    middle = inputs + lax.psum_scatter(
        jnp.dot(context_rows, w_out, preferred_element_type=jnp.float32).astype(jnp.bfloat16),
        "mp",
        scatter_dimension=0,
        tiled=True,
    ).astype(jnp.float32)
    normed_two = layer_norm(middle, ln2_gain, ln2_bias).astype(jnp.bfloat16)
    rows_two = lax.all_gather(normed_two, "mp", axis=0, tiled=True)
    up_pre = jnp.dot(rows_two, w_up, preferred_element_type=jnp.float32) + b_up
    hidden = jax.nn.gelu(up_pre, approximate=True).astype(jnp.bfloat16)
    output = (
        middle
        + (
            lax.psum_scatter(
                jnp.dot(hidden, w_down, preferred_element_type=jnp.float32).astype(jnp.bfloat16),
                "mp",
                scatter_dimension=0,
                tiled=True,
            ).astype(jnp.float32)
            + b_down
        )
    ).astype(jnp.bfloat16)
    grad_out = out_grad.astype(jnp.float32)
    bias_down = jnp.sum(grad_out, axis=0)
    rows_ffn = lax.all_gather(out_grad, "mp", axis=0, tiled=True)
    grad_hidden = jnp.einsum("nd,fd->nf", rows_ffn, w_down, preferred_element_type=jnp.float32)
    grad_down = jnp.einsum("nf,nd->fd", hidden, rows_ffn, preferred_element_type=jnp.float32)
    gelu_value, gelu_pull = jax.vjp(lambda pre_act: jax.nn.gelu(pre_act, approximate=True), up_pre)
    grad_up = gelu_pull(grad_hidden)[0].astype(jnp.bfloat16)
    bias_up = jnp.sum(grad_up, axis=0, dtype=jnp.float32)
    grad_up_weight = jnp.einsum("nd,nf->df", rows_two, grad_up, preferred_element_type=jnp.float32)
    grad_normed_two = lax.psum_scatter(
        jnp.einsum("nf,df->nd", grad_up, w_up, preferred_element_type=jnp.float32).astype(
            jnp.bfloat16
        ),
        "mp",
        scatter_dimension=0,
        tiled=True,
    ).astype(jnp.float32)
    norm_value_two, norm_pull_two = jax.vjp(layer_norm, middle, ln2_gain, ln2_bias)
    grad_mid_norm, gain_two, bias_two = norm_pull_two(grad_normed_two)
    grad_middle = grad_out + grad_mid_norm
    grad_attn = grad_middle.astype(jnp.bfloat16)
    rows_attn = lax.all_gather(grad_attn, "mp", axis=0, tiled=True)
    grad_context = jnp.einsum(
        "nd,ed->ne", rows_attn, w_out, preferred_element_type=jnp.float32
    ).astype(jnp.bfloat16)
    grad_out_weight = jnp.einsum(
        "ne,nd->ed", context_rows, rows_attn, preferred_element_type=jnp.float32
    )
    grad_joined = lax.map(
        lambda seq_items: attend_backward(seq_items, allowed, scaling),
        (joined_seq, grad_context.reshape(seq_count, SEQ, local_heads, HD), row_lse),
    )
    grad_joined = grad_joined.reshape(seq_count * SEQ, 3 * head_width)
    grad_joined_weight = jnp.einsum(
        "nd,ne->de", rows_one, grad_joined, preferred_element_type=jnp.float32
    )
    grad_normed_one = lax.psum_scatter(
        jnp.einsum("ne,de->nd", grad_joined, w_joined, preferred_element_type=jnp.float32).astype(
            jnp.bfloat16
        ),
        "mp",
        scatter_dimension=0,
        tiled=True,
    ).astype(jnp.float32)
    norm_value_one, norm_pull_one = jax.vjp(layer_norm, inputs, ln1_gain, ln1_bias)
    grad_in_norm, gain_one, bias_one = norm_pull_one(grad_normed_one)
    input_grad = grad_middle + grad_in_norm
    grad_joined_weight, grad_out_weight, grad_up_weight, bias_up, grad_down = (
        lax.psum(grad_joined_weight.astype(jnp.bfloat16), "dp").astype(jnp.float32),
        lax.psum(grad_out_weight.astype(jnp.bfloat16), "dp").astype(jnp.float32),
        lax.psum(grad_up_weight.astype(jnp.bfloat16), "dp").astype(jnp.float32),
        lax.psum(bias_up.astype(jnp.bfloat16), "dp").astype(jnp.float32),
        lax.psum(grad_down.astype(jnp.bfloat16), "dp").astype(jnp.float32),
    )
    gain_one, bias_one, gain_two, bias_two, bias_down = lax.psum(
        (gain_one, bias_one, gain_two, bias_two, bias_down), ("dp", "mp")
    )
    grad_query = grad_joined_weight[:, :head_width]
    grad_key = grad_joined_weight[:, head_width : 2 * head_width]
    grad_value = grad_joined_weight[:, 2 * head_width :]
    return (
        output,
        input_grad,
        gain_one,
        bias_one,
        grad_query,
        grad_key,
        grad_value,
        grad_out_weight,
        gain_two,
        bias_two,
        grad_up_weight,
        bias_up,
        grad_down,
        bias_down,
    )


def solution(mesh):
    in_specs = (
        P(("dp", "mp"), None),
        P(("dp", "mp"), None),
        P(),
        P(),
        P(None, "mp"),
        P(None, "mp"),
        P(None, "mp"),
        P("mp", None),
        P(),
        P(),
        P(None, "mp"),
        P("mp"),
        P("mp", None),
        P(),
        P("mp", None, None),
    )
    out_specs = (
        P(("dp", "mp"), None),
        P(("dp", "mp"), None),
        P(),
        P(),
        P(None, "mp"),
        P(None, "mp"),
        P(None, "mp"),
        P("mp", None),
        P(),
        P(),
        P(None, "mp"),
        P("mp"),
        P("mp", None),
        P(),
    )
    return jax.shard_map(
        per_device, mesh=mesh, in_specs=in_specs, out_specs=out_specs, check_vma=False
    )
```

profile of v0, /device:TPU:0, one launch (start us, length us, event | category | flops | bytes accessed | tf_op | source)
XLA Modules:
  0.0 1241.2 jit_solution(840713669255894146)
XLA Ops:
  22.0 52.6 %all-gather.5.cloned.1.call-done = bf16[2048,1024]{1,0:T(8,128)(2,1)} async-done(((bf16[1024,1024]{1,0:T(8,128)(2,1)}), bf16[2048,1024]{1,0:T(8,128)(2,1)}) %all-gather.5.cloned.1.call-update) | async-done | bytes 4194320 | tf_op jit(solution)/shard_map/all_gather | solution.py:107
  86.1 16.3 %reshape.244 = bf16[2,1024,3,8,64]{4,3,2,1,0:T(8,128)(2,1)} reshape(bf16[2048,1536]{1,0:T(8,128)(2,1)} %convolution_convert_fusion.2) | data formatting | bytes 12582912 | tf_op jit(solution)/shard_map/reshape | solution.py:109
  102.3 14.0 %copy.56 = bf16[2,1024,3,8,64]{1,4,3,2,0:T(8,128)(2,1)} copy(bf16[2,1024,3,8,64]{4,3,2,1,0:T(8,128)(2,1)} %reshape.244) | data formatting | bytes 12582912
  116.4 113.5 %while.24 = (s32[]{:T(128)}, bf16[2,1024,8,64]{1,3,2,0:T(8,128)(2,1)}, f32[2,8,1024]{2,1,0:T(8,128)S(1)}, bf16[2,1024,3,8,64]{1,4,3,2,0:T(8,128)(2,1)}, pred[8,1024,16]{1,2,0:T(8,128)(4,1)S(1)}, /*index=5*/s32[]{:T(128)}) while((s32[]{:T(128)}, bf16[2,1024,8,64]{1,3,2,0:T(8,128)(2,1)}, f32[2,8,1024]{2,1,0:T(8,128)S(1)}, ...), condition=%wide.region_6.7_spmd.clone, body=%wide.region_3.6_spmd.clone.sunk | while | flops 2248663040 | bytes 279576704 | solution.py:110
  131.9 14.7 %fusion.102 = f32[8,1024]{1,0:T(8,128)S(1)} fusion(f32[8,1024,1024]{1,2,0:T(8,128)} %get-tuple-element.264, f32[8,1024]{1,0:T(8,128)S(1)} %get-tuple-element.265, pred[8,1024,16]{1,2,0:T(8,128)(4,1)S(1)} %get-tuple-element.292), kind=kLoop, calls=%fused_computation.6.clone.1 | loop fusion | flops 33546240 | bytes 33751040 | tf_op jit(solution)/shard_map/while/body/eval_jaxpr/reduce_sum | solution.py:43
  188.4 14.7 %fusion.102 = f32[8,1024]{1,0:T(8,128)S(1)} fusion(f32[8,1024,1024]{1,2,0:T(8,128)} %get-tuple-element.264, f32[8,1024]{1,0:T(8,128)S(1)} %get-tuple-element.265, pred[8,1024,16]{1,2,0:T(8,128)(4,1)S(1)} %get-tuple-element.292), kind=kLoop, calls=%fused_computation.6.clone.1 | loop fusion | flops 33546240 | bytes 33751040 | tf_op jit(solution)/shard_map/while/body/eval_jaxpr/reduce_sum | solution.py:43
  240.1 54.4 %reduce-scatter.5.cloned.1.call-done = bf16[1024,1024]{1,0:T(8,128)(2,1)} async-done(((bf16[2048,1024]{1,0:T(8,128)(2,1)}), bf16[1024,1024]{1,0:T(8,128)(2,1)}) %reduce-scatter.5.cloned.1.call-update) | async-done | bytes 2097168 | tf_op jit(solution)/shard_map/reduce_scatter | solution.py:114
  300.9 56.3 %all-gather.7.cloned.1.call-done = bf16[2048,1024]{1,0:T(8,128)(2,1)} async-done(((bf16[1024,1024]{1,0:T(8,128)(2,1)}), bf16[2048,1024]{1,0:T(8,128)(2,1)}) %all-gather.7.cloned.1.call-update) | async-done | bytes 4194320 | tf_op jit(solution)/shard_map/all_gather | solution.py:121
  357.2 20.6 %multiply_convert_fusion.3 = (bf16[2048,2048]{1,0:T(8,128)(2,1)}, f32[2048,2048]{1,0:T(8,128)}) fusion(f32[2048]{0:T(1024)S(1)} %copy-done.44, bf16[2048,1024]{1,0:T(8,128)(2,1)} %all-gather.7.cloned.1.call-done, bf16[1024,2048]{1,0:T(8,128)(2,1)} %param.29), kind=kOutput, calls=%fused_computation.50 | convolution fusion | flops 8631877632 | bytes 33562624 | tf_op jit(solution)/shard_map/dot_general | solution.py:122
  377.8 37.6 %all-gather.9.cloned.1.call-done = bf16[2048,1024]{1,0:T(8,128)(2,1)} async-done(((bf16[1024,1024]{1,0:T(8,128)(2,1)}), bf16[2048,1024]{1,0:T(8,128)(2,1)}) %all-gather.9.cloned.1.call-update) | async-done | bytes 4194320 | tf_op jit(solution)/shard_map/all_gather | solution.py:138
  415.4 28.1 %fusion.55 = (bf16[2048]{0:T(1024)(128)(2,1)}, bf16[2048,2048]{1,0:T(8,128)(2,1)}) fusion(f32[2048,2048]{1,0:T(8,128)} %get-tuple-element.193, f32[2048]{0:T(1024)S(1)} %copy-done.44, bf16[2048,1024]{1,0:T(8,128)(2,1)} %all-gather.9.cloned.1.call-done, bf16[2048,1024]{1,0:T(8,128)(2,1)} %param.31), kind=kOutput, calls=%fused_computation.120 | convolution fusion | flops 8682207232 | bytes 33566720 | tf_op jit(solution)/shard_map/nd,fd->nf/dot_general | solution.py:139
  470.4 40.5 %reduce-scatter.9.cloned.1.call-done = bf16[1024,1024]{1,0:T(8,128)(2,1)} async-done(((bf16[2048,1024]{1,0:T(8,128)(2,1)}), bf16[1024,1024]{1,0:T(8,128)(2,1)}) %reduce-scatter.9.cloned.1.call-update) | async-done | bytes 2097168 | tf_op jit(solution)/shard_map/reduce_scatter | solution.py:145
  515.3 52.0 %reduce-scatter.7.cloned.1.call-done = bf16[1024,1024]{1,0:T(8,128)(2,1)} async-done(((bf16[2048,1024]{1,0:T(8,128)(2,1)}), bf16[1024,1024]{1,0:T(8,128)(2,1)}) %reduce-scatter.7.cloned.1.call-update) | async-done | bytes 2097168 | tf_op jit(solution)/shard_map/reduce_scatter | solution.py:127
  576.9 14.7 %convolution_convert_fusion.9 = bf16[2048,1024]{1,0:T(8,128)(2,1)} fusion(bf16[2048,2048]{1,0:T(8,128)(2,1)} %get-tuple-element.192, bf16[2048,1024]{1,0:T(8,128)(2,1)} %all-gather.9.cloned.1.call-done), kind=kOutput, calls=%fused_computation.90 | convolution fusion | flops 8592031744 | bytes 16777216 | tf_op jit(solution)/shard_map/nf,nd->fd/dot_general | solution.py:140
  604.7 29.0 %all-gather.11.cloned.1.call-done = bf16[2048,1024]{1,0:T(8,128)(2,1)} async-done(((bf16[1024,1024]{1,0:T(8,128)(2,1)}), bf16[2048,1024]{1,0:T(8,128)(2,1)}) %all-gather.11.cloned.1.call-update) | async-done | bytes 4194320 | tf_op jit(solution)/shard_map/all_gather | solution.py:157
  647.3 213.0 %while.25 = (s32[]{:T(128)}, bf16[2,1024,3,8,64]{1,4,3,2,0:T(8,128)(2,1)}, bf16[2,1024,3,8,64]{1,4,3,2,0:T(8,128)(2,1)}, f32[2,8,1024]{2,1,0:T(8,128)S(1)}, bf16...) while((s32[]{:T(128)}, ...), condition=%wide.region_16.17_spmd.clone, body=%wide.region_14.16_spmd.clone.sunk | while | flops 5481422848 | bytes 287768704 | solution.py:164
  662.9 23.8 %multiply_reduce_fusion.3 = (f32[8,1024]{1,0:T(8,128)S(1)}, f32[8,1024,1024]{1,2,0:T(8,128)}) fusion(f32[8,1024,1024]{1,2,0:T(8,128)} %fusion.108, f32[8,1024]{1,0:T(8,128)S(1)} %dynamic-slice_bitcast_fusion.8, pred[8,1024,16]{1,2,0:T(8,128)(4,1)S(1)} %get-tuple-element.313, bf16[1024,3,8,64]{0,3,2,1:T(8,128)(2,1)S(1)} %dynamic-slice_bitcast_fusion.7, ...), kind=kOutput, calls=%fused_computation.17.clone.1 | convolution fusion | flops 1115676672 | bytes 69402624 | tf_op jit(solution)/shard_map/while/body/eval_jaxpr/qhd,khd->hqk/dot_general | solution.py:65
  686.7 33.3 %multiply_convert_fusion.5 = (bf16[8,1024,1024]{1,2,0:T(8,128)(2,1)}, bf16[8,1024,1024]{1,2,0:T(8,128)(2,1)}) fusion(f32[8,1024,1024]{1,2,0:T(8,128)} %get-tuple-element.272, f32[8,1024,1024]{1,2,0:T(8,128)} %fusion.108, f32[8,1024]{1,0:T(8,128)S(1)} %get-tuple-element.273, f32[8,1024]{1,0:T(8,128)S(1)} %dynamic-slice_bitcast_fusion.8, ...), kind=kLoop, calls=%fused_computation.16.clone.1 | loop fusion | flops 58720256 | bytes 100859904 | tf_op jit(solution)/shard_map/while/body/eval_jaxpr/convert_element_type | solution.py:69
  769.2 23.8 %multiply_reduce_fusion.3 = (f32[8,1024]{1,0:T(8,128)S(1)}, f32[8,1024,1024]{1,2,0:T(8,128)}) fusion(f32[8,1024,1024]{1,2,0:T(8,128)} %fusion.108, f32[8,1024]{1,0:T(8,128)S(1)} %dynamic-slice_bitcast_fusion.8, pred[8,1024,16]{1,2,0:T(8,128)(4,1)S(1)} %get-tuple-element.313, bf16[1024,3,8,64]{0,3,2,1:T(8,128)(2,1)S(1)} %dynamic-slice_bitcast_fusion.7, ...), kind=kOutput, calls=%fused_computation.17.clone.1 | convolution fusion | flops 1115676672 | bytes 69402624 | tf_op jit(solution)/shard_map/while/body/eval_jaxpr/qhd,khd->hqk/dot_general | solution.py:65
  793.1 33.3 %multiply_convert_fusion.5 = (bf16[8,1024,1024]{1,2,0:T(8,128)(2,1)}, bf16[8,1024,1024]{1,2,0:T(8,128)(2,1)}) fusion(f32[8,1024,1024]{1,2,0:T(8,128)} %get-tuple-element.272, f32[8,1024,1024]{1,2,0:T(8,128)} %fusion.108, f32[8,1024]{1,0:T(8,128)S(1)} %get-tuple-element.273, f32[8,1024]{1,0:T(8,128)S(1)} %dynamic-slice_bitcast_fusion.8, ...), kind=kLoop, calls=%fused_computation.16.clone.1 | loop fusion | flops 58720256 | bytes 100859904 | tf_op jit(solution)/shard_map/while/body/eval_jaxpr/convert_element_type | solution.py:69
  903.7 35.2 %psum.77 = bf16[2048]{0:T(1024)(128)(2,1)S(1)} all-reduce(bf16[2048]{0:T(1024)(128)(2,1)S(1)} %copy-done.38), channel_id=1, replica_groups=mesh['dp'=16,'mp'=2] {'dp'}, use_global_device_ids=true, to_apply=%region_32.33 | all-reduce | flops 2048 | bytes 8192 | tf_op jit(solution)/shard_map/psum | solution.py:187
  939.5 186.7 %all-reduce.4.cloned.1.call-done = (bf16[1024,1536]{1,0:T(8,128)(2,1)}, bf16[512,1024]{1,0:T(8,128)(2,1)}, bf16[1024,2048]{1,0:T(8,128)(2,1)}, bf16[2048,1024]{1,0:T(8,128)(2,1)}) async-done(((bf16[1024,1536]{1,0:T(8,128)(2,1)}, bf16[512,1024]{1,0:T(8,128)(2,1)}, bf16[1024,2048]{1,0:T(8,128)(2,1)}, bf16[2048,1024]{1,0:T(8,128)(2,1)}), (bf16[1024,1536]{1,0:T(8,128)(2,1)}, bf16[512,1024]{1,0:T(8,128)(2,1)}, ...) | async-done | bytes 12582928 | tf_op jit(solution)/shard_map/psum | solution.py:184
  1143.3 40.2 %reduce-scatter.11.cloned.1.call-done = bf16[1024,1024]{1,0:T(8,128)(2,1)} async-done(((bf16[2048,1024]{1,0:T(8,128)(2,1)}), bf16[1024,1024]{1,0:T(8,128)(2,1)}) %reduce-scatter.11.cloned.1.call-update) | async-done | bytes 2097168 | tf_op jit(solution)/shard_map/reduce_scatter | solution.py:172
  1194.4 39.8 %all-reduce = (f32[1024]{0:T(1024)}, f32[1024]{0:T(1024)}, f32[1024]{0:T(1024)}, f32[1024]{0:T(1024)}, f32[1024]{0:T(1024)}) all-reduce(f32[1024]{0:T(1024)S(1)} %get-tuple-element.140, f32[1024]{0:T(1024)S(1)} %get-tuple-element.143, f32[1024]{0:T(1024)S(1)} %copy-done.34, ...), channel_id=1, replica_groups=mesh['dp'=16,'mp'=2] {'dp','mp'}, use_global_device_ids=true, to_apply=%region_21.22 | all-reduce | flops 5120 | bytes 40960 | tf_op jit(solution)/shard_map/psum | solution.py:190
  (190 shorter events, 363.7 us)
Async XLA Ops:
  7.2 228.5 %copy-start = (bf16[512,1024]{1,0:T(8,128)(2,1)S(1)}, bf16[512,1024]{1,0:T(8,128)(2,1)}, u32[]{:S(2)}) copy-start(bf16[512,1024]{1,0:T(8,128)(2,1)} %param.26) | copy-start | bytes 3145732
  7.2 67.4 %all-gather.5.cloned.1.call-start = ((), (), s32[]{:S(2)}) async-start(), calls=%async_computation.4 | async-start | bytes 6291456 | tf_op jit(solution)/shard_map/all_gather | solution.py:107
  15.1 279.5 %reduce-scatter.5.cloned.1.call-start = ((), (), s32[]{:S(2)}) async-start(), calls=%async_computation.5 | async-start | bytes 6291456 | tf_op jit(solution)/shard_map/reduce_scatter | solution.py:114
  131.9 20.3 %copy-start.2 = (f32[8,1024,1024]{1,2,0:T(8,128)S(1)}, f32[8,1024,1024]{1,2,0:T(8,128)}, u32[]{:S(2)}) copy-start(f32[8,1024,1024]{1,2,0:T(8,128)} %get-tuple-element.264) | copy-start | bytes 100663296 | tf_op jit(solution)/shard_map/while
  240.0 54.5 %copy-start.5 = (bf16[1024,1024]{1,0:T(8,128)(2,1)S(1)}, bf16[1024,1024]{1,0:T(8,128)(2,1)}, u32[]{:S(2)}) copy-start(bf16[1024,1024]{1,0:T(8,128)(2,1)} %param.19) | copy-start | bytes 6291460
  240.1 57.8 %copy-start.33 = (f32[1024]{0:T(1024)S(1)}, f32[1024]{0:T(1024)}, u32[]{:S(2)}) copy-start(f32[1024]{0:T(1024)} %param.27) | copy-start | bytes 12292
  240.1 57.8 %copy-start.37 = (f32[1024]{0:T(1024)S(1)}, f32[1024]{0:T(1024)}, u32[]{:S(2)}) copy-start(f32[1024]{0:T(1024)} %param.28) | copy-start | bytes 12292
  240.1 117.1 %all-gather.7.cloned.1.call-start = ((), (), s32[]{:S(2)}) async-start(), calls=%async_computation.6 | async-start | bytes 6291456 | tf_op jit(solution)/shard_map/all_gather | solution.py:121
  297.8 59.3 %copy-start.44 = (f32[2048]{0:T(1024)S(1)}, f32[2048]{0:T(1024)}, u32[]{:S(2)}) copy-start(f32[2048]{0:T(1024)} %param.30) | copy-start | bytes 24580
  300.2 115.2 %all-gather.9.cloned.1.call-start = ((), (), s32[]{:S(2)}) async-start(), calls=%async_computation.8 | async-start | bytes 6291456 | tf_op jit(solution)/shard_map/all_gather | solution.py:138
  300.8 210.1 %reduce-scatter.9.cloned.1.call-start = ((), (), s32[]{:S(2)}) async-start(), calls=%async_computation.9 | async-start | bytes 6291456 | tf_op jit(solution)/shard_map/reduce_scatter | solution.py:145
  415.4 28.1 %copy-start.41 = (bf16[1024,2048]{1,0:T(8,128)(2,1)S(1)}, bf16[1024,2048]{1,0:T(8,128)(2,1)}, u32[]{:S(2)}) copy-start(bf16[1024,2048]{1,0:T(8,128)(2,1)} %param.29) | copy-start | bytes 12582916
  456.4 110.9 %reduce-scatter.7.cloned.1.call-start = ((), (), s32[]{:S(2)}) async-start(), calls=%async_computation.7 | async-start | bytes 6291456 | tf_op jit(solution)/shard_map/reduce_scatter | solution.py:127
  470.3 97.0 %copy-start.40 = (f32[1024]{0:T(1024)S(1)}, f32[1024]{0:T(1024)}, u32[]{:S(2)}) copy-start(f32[1024]{0:T(1024)} %param.32) | copy-start | bytes 12292
  470.3 163.4 %all-gather.11.cloned.1.call-start = ((), (), s32[]{:S(2)}) async-start(), calls=%async_computation.10 | async-start | bytes 6291456 | tf_op jit(solution)/shard_map/all_gather | solution.py:157
  576.8 549.4 %all-reduce.4.cloned.1.call-start = ((), (), s32[]{:S(2)}) async-start(), calls=%async_computation.12 | async-start | bytes 25165824 | tf_op jit(solution)/shard_map/psum | solution.py:184
  891.1 292.4 %reduce-scatter.11.cloned.1.call-start = ((), (), s32[]{:S(2)}) async-start(), calls=%async_computation.11 | async-start | bytes 6291456 | tf_op jit(solution)/shard_map/reduce_scatter | solution.py:172
  1140.3 43.2 %copy-start.6 = (bf16[1024,1024]{1,0:T(8,128)(2,1)S(1)}, bf16[1024,1024]{1,0:T(8,128)(2,1)}, u32[]{:S(2)}) copy-start(bf16[1024,1024]{1,0:T(8,128)(2,1)} %param.19) | copy-start | bytes 6291460
  1140.3 43.2 %copy-start.24 = (f32[1024]{0:T(1024)S(1)}, f32[1024]{0:T(1024)}, u32[]{:S(2)}) copy-start(f32[1024]{0:T(1024)} %copy-done.23) | copy-start | bytes 12292
  1140.3 43.2 %copy-start.28 = (f32[1024]{0:T(1024)S(1)}, f32[1024]{0:T(1024)}, u32[]{:S(2)}) copy-start(f32[1024]{0:T(1024)} %param.21) | copy-start | bytes 12292
  1143.3 43.3 %copy-start.32 = (f32[1024]{0:T(1024)S(1)}, f32[1024]{0:T(1024)}, u32[]{:S(2)}) copy-start(f32[1024]{0:T(1024)} %copy-done.31) | copy-start | bytes 12292
  1143.3 43.4 %copy-start.26 = (f32[1024]{0:T(1024)S(1)}, f32[1024]{0:T(1024)}, u32[]{:S(2)}) copy-start(f32[1024]{0:T(1024)} %copy-done.25) | copy-start | bytes 12292
  1143.3 47.3 %copy-start.30 = (f32[1024]{0:T(1024)S(1)}, f32[1024]{0:T(1024)}, u32[]{:S(2)}) copy-start(f32[1024]{0:T(1024)} %copy-done.29) | copy-start | bytes 12292
  1190.6 43.6 %copy-start.1 = (bf16[512,1024]{1,0:T(8,128)(2,1)S(1)}, bf16[512,1024]{1,0:T(8,128)(2,1)}, u32[]{:S(2)}) copy-start(bf16[512,1024]{1,0:T(8,128)(2,1)} %param.26) | copy-start | bytes 3145732
  (32 other events, 186.0 us)
Sparse Core Ops, SparseCore 0:
  15.2 59.4 all-gather.4
  240.2 54.3 reduce-scatter.4
  300.4 56.7 all-gather.6
  358.6 56.7 all-gather.8
  456.5 54.3 reduce-scatter.8
  513.0 54.2 reduce-scatter.6
  576.9 56.7 all-gather.10
  891.2 234.9 all-reduce.3
  1129.1 54.3 reduce-scatter.10
where the time goes:
time: 1250 us; the launch traced here: 1240 us
  waiting for transfers between devices  550 us (44%)
  matrix products  335 us (27%)
  other arithmetic  172 us (14%)
  local copies, waits for them, and re-layouts  93.5 us (7%)
  blocking collectives  75.1 us (6%)
  between operations  14.8 us (1%)
    psum x1, waiting for transfers between devices, per_device(): lax.psum(grad_joined_weight.astype(jnp.bfloat16), 'dp').astype(jnp.float32)  187 us
    convert_element_type x2, other arithmetic, attend_backward(): grad_scores = (attn_probs * (grad_probs - row_inner)).astype(jnp.bfloat16)  66.6 us
    all_gather x1, waiting for transfers between devices, per_device(): rows_two = lax.all_gather(normed_two, 'mp', axis=0, tiled=True)  56.3 us
    reduce_scatter x1, waiting for transfers between devices, per_device(): lax.psum_scatter(jnp.dot(context_rows, w_out, preferred_element_type=jnp....  54.4 us
    all_gather x1, waiting for transfers between devices, per_device(): rows_one = lax.all_gather(normed_one, 'mp', axis=0, tiled=True)  52.6 us
    reduce_scatter x1, waiting for transfers between devices, per_device(): lax.psum_scatter(jnp.dot(hidden, w_down, preferred_element_type=jnp.float...  52 us
    dot_general x2, matrix products, attend_backward(): jnp.einsum('qhd,khd->hqk', grad_context, value_rows, preferred_element_ty...  47.7 us
    reduce_scatter x1, waiting for transfers between devices, per_device(): lax.psum_scatter(jnp.einsum('nf,df->nd', grad_up, w_up, preferred_element...  40.5 us
  transfers between devices with their start and end apart: 9, of which 9 were waited for; matrix products, arithmetic and copies ran while one was open for 8% of the time, Pallas kernels for 0%

commit v1 on v0

--- a/solution.py
+++ b/solution.py
@@ -6,6 +6,18 @@
 HD = 64
 BLOCK = 64
 SEQ = 1024
+
+
+def doubled_up(value, axis, dim):
+    ways, here, step = (lax.axis_size(axis), lax.axis_index(axis), value.shape[dim])
+    line, have = (value, 1)
+    while have < ways:
+        line = jnp.concatenate(
+            [line, lax.ppermute(line, axis, [(d, (d - have) % ways) for d in range(ways)])],
+            axis=dim,
+        )
+        have = 2 * have
+    return jnp.roll(line, here * step, axis=dim)
 
 
 def layer_norm(values, norm_gain, norm_bias):
@@ -118,7 +130,7 @@
         tiled=True,
     ).astype(jnp.float32)
     normed_two = layer_norm(middle, ln2_gain, ln2_bias).astype(jnp.bfloat16)
-    rows_two = lax.all_gather(normed_two, "mp", axis=0, tiled=True)
+    rows_two = doubled_up(normed_two, "mp", 0)
     up_pre = jnp.dot(rows_two, w_up, preferred_element_type=jnp.float32) + b_up
     hidden = jax.nn.gelu(up_pre, approximate=True).astype(jnp.bfloat16)
     output = (

time: 1250 us -> 1240 us (level)
    ppermute x0 -> x1, waiting for transfers between devices: none -> 82.6 us  [doubled_up(): lax.ppermute(line, axis, [(d, (d - have) % ways) for d in range(ways)])]
    all_gather x1 -> x0, waiting for transfers between devices: 56.3 us -> none  [per_device(): rows_two = lax.all_gather(normed_two, 'mp', axis=0, tiled=True)]
    all_gather x1, waiting for transfers between devices: 37.6 us -> 0.01 us  [per_device(): rows_ffn = lax.all_gather(out_grad, 'mp', axis=0, tiled=True)]
    unnamed x93 -> x97, local copies, waits for them, and re-layouts: 31.5 us -> 33.4 us
  transfers between devices with their start and end apart: 9 -> 9, of which waited for: 9 -> 8; matrix products, arithmetic and copies ran while one was open for 8% -> 9% of each run, Pallas kernels for 0% -> 0%
where the time goes in v1:
time: 1240 us; the launch traced here: 1230 us
  waiting for transfers between devices  538 us (43%)
  matrix products  331 us (27%)
  other arithmetic  179 us (14%)
  local copies, waits for them, and re-layouts  95.4 us (8%)
  blocking collectives  75.1 us (6%)
  between operations  15.1 us (1%)
    psum x1, waiting for transfers between devices, per_device(): lax.psum(grad_joined_weight.astype(jnp.bfloat16), 'dp').astype(jnp.float32)  187 us
    ppermute x1, waiting for transfers between devices, doubled_up(): lax.ppermute(line, axis, [(d, (d - have) % ways) for d in range(ways)])  82.6 us
    convert_element_type x2, other arithmetic, attend_backward(): grad_scores = (attn_probs * (grad_probs - row_inner)).astype(jnp.bfloat16)  66.6 us
    reduce_scatter x1, waiting for transfers between devices, per_device(): lax.psum_scatter(jnp.dot(context_rows, w_out, preferred_element_type=jnp....  54.4 us
    all_gather x1, waiting for transfers between devices, per_device(): rows_one = lax.all_gather(normed_one, 'mp', axis=0, tiled=True)  52.6 us
    reduce_scatter x1, waiting for transfers between devices, per_device(): lax.psum_scatter(jnp.dot(hidden, w_down, preferred_element_type=jnp.float...  52 us
    dot_general x2, matrix products, attend_backward(): jnp.einsum('qhd,khd->hqk', grad_context, value_rows, preferred_element_ty...  47.7 us
    reduce_scatter x1, waiting for transfers between devices, per_device(): lax.psum_scatter(jnp.einsum('nf,df->nd', grad_up, w_up, preferred_element...  40.5 us
  transfers between devices with their start and end apart: 9, of which 8 were waited for; matrix products, arithmetic and copies ran while one was open for 9% of the time, Pallas kernels for 0%

profile of v1, /device:TPU:0, one launch (start us, length us, event | category | flops | bytes accessed | tf_op | source)
XLA Modules:
  0.0 1234.6 jit_solution(4419521875692817850)
XLA Ops:
  22.0 52.6 %all-gather.4.cloned.1.call-done = bf16[2048,1024]{1,0:T(8,128)(2,1)} async-done(((bf16[1024,1024]{1,0:T(8,128)(2,1)}), bf16[2048,1024]{1,0:T(8,128)(2,1)}) %all-gather.4.cloned.1.call-update) | async-done | bytes 4194320 | tf_op jit(solution)/shard_map/all_gather | solution.py:119
  86.1 16.3 %reshape.244 = bf16[2,1024,3,8,64]{4,3,2,1,0:T(8,128)(2,1)} reshape(bf16[2048,1536]{1,0:T(8,128)(2,1)} %convolution_convert_fusion.2) | data formatting | bytes 12582912 | tf_op jit(solution)/shard_map/reshape | solution.py:121
  102.3 14.0 %copy.56 = bf16[2,1024,3,8,64]{1,4,3,2,0:T(8,128)(2,1)} copy(bf16[2,1024,3,8,64]{4,3,2,1,0:T(8,128)(2,1)} %reshape.244) | data formatting | bytes 12582912
  116.4 113.5 %while.24 = (s32[]{:T(128)}, bf16[2,1024,8,64]{1,3,2,0:T(8,128)(2,1)}, f32[2,8,1024]{2,1,0:T(8,128)S(1)}, bf16[2,1024,3,8,64]{1,4,3,2,0:T(8,128)(2,1)}, pred[8,1024,16]{1,2,0:T(8,128)(4,1)S(1)}, /*index=5*/s32[]{:T(128)}) while((s32[]{:T(128)}, bf16[2,1024,8,64]{1,3,2,0:T(8,128)(2,1)}, f32[2,8,1024]{2,1,0:T(8,128)S(1)}, ...), condition=%wide.region_6.7_spmd.clone, body=%wide.region_3.6_spmd.clone.sunk | while | flops 2248663040 | bytes 279576704 | solution.py:122
  131.9 14.7 %fusion.105 = f32[8,1024]{1,0:T(8,128)S(1)} fusion(f32[8,1024,1024]{1,2,0:T(8,128)} %get-tuple-element.264, f32[8,1024]{1,0:T(8,128)S(1)} %get-tuple-element.265, pred[8,1024,16]{1,2,0:T(8,128)(4,1)S(1)} %get-tuple-element.292), kind=kLoop, calls=%fused_computation.6.clone.1 | loop fusion | flops 33546240 | bytes 33751040 | tf_op jit(solution)/shard_map/while/body/eval_jaxpr/reduce_sum | solution.py:55
  188.4 14.7 %fusion.105 = f32[8,1024]{1,0:T(8,128)S(1)} fusion(f32[8,1024,1024]{1,2,0:T(8,128)} %get-tuple-element.264, f32[8,1024]{1,0:T(8,128)S(1)} %get-tuple-element.265, pred[8,1024,16]{1,2,0:T(8,128)(4,1)S(1)} %get-tuple-element.292), kind=kLoop, calls=%fused_computation.6.clone.1 | loop fusion | flops 33546240 | bytes 33751040 | tf_op jit(solution)/shard_map/while/body/eval_jaxpr/reduce_sum | solution.py:55
  240.1 54.4 %reduce-scatter.5.cloned.1.call-done = bf16[1024,1024]{1,0:T(8,128)(2,1)} async-done(((bf16[2048,1024]{1,0:T(8,128)(2,1)}), bf16[1024,1024]{1,0:T(8,128)(2,1)}) %reduce-scatter.5.cloned.1.call-update) | async-done | bytes 2097168 | tf_op jit(solution)/shard_map/reduce_scatter | solution.py:126
  300.6 82.6 %collective-permute-done = bf16[1024,1024]{1,0:T(8,128)(2,1)} collective-permute-done((bf16[1024,1024]{1,0:T(8,128)(2,1)}, bf16[1024,1024]{1,0:T(8,128)(2,1)}, u32[]{:S(2)}, u32[]{:S(2)}) %collective-permute-start) | collective-permute-done | bytes 2097184 | tf_op jit(solution)/shard_map/ppermute | solution.py:16
  392.2 16.4 %multiply_convert_fusion.3 = (bf16[2048,2048]{1,0:T(8,128)(2,1)}, f32[2048,2048]{1,0:T(8,128)}) fusion(f32[2048]{0:T(1024)S(1)} %copy-done.46, bf16[2048,1024]{1,0:T(8,128)(2,1)S(1)} %fusion.46, bf16[1024,2048]{1,0:T(8,128)(2,1)S(1)} %copy-done.43), kind=kOutput, calls=%fused_computation.50 | convolution fusion | flops 8631877632 | bytes 33562624 | tf_op jit(solution)/shard_map/dot_general | solution.py:134
  408.6 28.0 %fusion.58 = (bf16[2048]{0:T(1024)(128)(2,1)}, bf16[2048,2048]{1,0:T(8,128)(2,1)}) fusion(f32[2048,2048]{1,0:T(8,128)} %get-tuple-element.193, f32[2048]{0:T(1024)S(1)} %copy-done.46, bf16[2048,1024]{1,0:T(8,128)(2,1)} %all-gather.6.cloned.1.call-done, bf16[2048,1024]{1,0:T(8,128)(2,1)} %param.31), kind=kOutput, calls=%fused_computation.127 | convolution fusion | flops 8682207232 | bytes 33566720 | tf_op jit(solution)/shard_map/nd,fd->nf/dot_general | solution.py:151
  449.6 13.8 %convolution_convert_fusion.7 = bf16[2048,1024]{1,0:T(8,128)(2,1)} fusion(bf16[2048,2048]{1,0:T(8,128)(2,1)} %get-tuple-element.192, bf16[2048,1024]{1,0:T(8,128)(2,1)} %param.31), kind=kOutput, calls=%fused_computation.95 | convolution fusion | flops 8592031744 | bytes 16777216 | tf_op jit(solution)/shard_map/dot_general | solution.py:140
  463.5 40.5 %reduce-scatter.9.cloned.1.call-done = bf16[1024,1024]{1,0:T(8,128)(2,1)} async-done(((bf16[2048,1024]{1,0:T(8,128)(2,1)}), bf16[1024,1024]{1,0:T(8,128)(2,1)}) %reduce-scatter.9.cloned.1.call-update) | async-done | bytes 2097168 | tf_op jit(solution)/shard_map/reduce_scatter | solution.py:157
  508.5 52.0 %reduce-scatter.7.cloned.1.call-done = bf16[1024,1024]{1,0:T(8,128)(2,1)} async-done(((bf16[2048,1024]{1,0:T(8,128)(2,1)}), bf16[1024,1024]{1,0:T(8,128)(2,1)}) %reduce-scatter.7.cloned.1.call-update) | async-done | bytes 2097168 | tf_op jit(solution)/shard_map/reduce_scatter | solution.py:139
  570.0 14.7 %convolution_convert_fusion.9 = bf16[2048,1024]{1,0:T(8,128)(2,1)} fusion(bf16[2048,2048]{1,0:T(8,128)(2,1)} %get-tuple-element.192, bf16[2048,1024]{1,0:T(8,128)(2,1)} %all-gather.6.cloned.1.call-done), kind=kOutput, calls=%fused_computation.97 | convolution fusion | flops 8592031744 | bytes 16777216 | tf_op jit(solution)/shard_map/nf,nd->fd/dot_general | solution.py:152
  597.8 29.0 %all-gather.8.cloned.1.call-done = bf16[2048,1024]{1,0:T(8,128)(2,1)} async-done(((bf16[1024,1024]{1,0:T(8,128)(2,1)}), bf16[2048,1024]{1,0:T(8,128)(2,1)}) %all-gather.8.cloned.1.call-update) | async-done | bytes 4194320 | tf_op jit(solution)/shard_map/all_gather | solution.py:169
  640.5 213.0 %while.25 = (s32[]{:T(128)}, bf16[2,1024,3,8,64]{1,4,3,2,0:T(8,128)(2,1)}, bf16[2,1024,3,8,64]{1,4,3,2,0:T(8,128)(2,1)}, f32[2,8,1024]{2,1,0:T(8,128)S(1)}, bf16...) while((s32[]{:T(128)}, ...), condition=%wide.region_16.17_spmd.clone, body=%wide.region_14.16_spmd.clone.sunk | while | flops 5481422848 | bytes 287768704 | solution.py:176
  656.0 23.8 %multiply_reduce_fusion.3 = (f32[8,1024]{1,0:T(8,128)S(1)}, f32[8,1024,1024]{1,2,0:T(8,128)}) fusion(f32[8,1024,1024]{1,2,0:T(8,128)} %fusion.111, f32[8,1024]{1,0:T(8,128)S(1)} %dynamic-slice_bitcast_fusion.8, pred[8,1024,16]{1,2,0:T(8,128)(4,1)S(1)} %get-tuple-element.313, bf16[1024,3,8,64]{0,3,2,1:T(8,128)(2,1)S(1)} %dynamic-slice_bitcast_fusion.7, ...), kind=kOutput, calls=%fused_computation.17.clone.1 | convolution fusion | flops 1115676672 | bytes 69402624 | tf_op jit(solution)/shard_map/while/body/eval_jaxpr/qhd,khd->hqk/dot_general | solution.py:77
  679.9 33.3 %multiply_convert_fusion.5 = (bf16[8,1024,1024]{1,2,0:T(8,128)(2,1)}, bf16[8,1024,1024]{1,2,0:T(8,128)(2,1)}) fusion(f32[8,1024,1024]{1,2,0:T(8,128)} %get-tuple-element.272, f32[8,1024,1024]{1,2,0:T(8,128)} %fusion.111, f32[8,1024]{1,0:T(8,128)S(1)} %get-tuple-element.273, f32[8,1024]{1,0:T(8,128)S(1)} %dynamic-slice_bitcast_fusion.8, ...), kind=kLoop, calls=%fused_computation.16.clone.1 | loop fusion | flops 58720256 | bytes 100859904 | tf_op jit(solution)/shard_map/while/body/eval_jaxpr/convert_element_type | solution.py:81
  762.4 23.8 %multiply_reduce_fusion.3 = (f32[8,1024]{1,0:T(8,128)S(1)}, f32[8,1024,1024]{1,2,0:T(8,128)}) fusion(f32[8,1024,1024]{1,2,0:T(8,128)} %fusion.111, f32[8,1024]{1,0:T(8,128)S(1)} %dynamic-slice_bitcast_fusion.8, pred[8,1024,16]{1,2,0:T(8,128)(4,1)S(1)} %get-tuple-element.313, bf16[1024,3,8,64]{0,3,2,1:T(8,128)(2,1)S(1)} %dynamic-slice_bitcast_fusion.7, ...), kind=kOutput, calls=%fused_computation.17.clone.1 | convolution fusion | flops 1115676672 | bytes 69402624 | tf_op jit(solution)/shard_map/while/body/eval_jaxpr/qhd,khd->hqk/dot_general | solution.py:77
  786.2 33.3 %multiply_convert_fusion.5 = (bf16[8,1024,1024]{1,2,0:T(8,128)(2,1)}, bf16[8,1024,1024]{1,2,0:T(8,128)(2,1)}) fusion(f32[8,1024,1024]{1,2,0:T(8,128)} %get-tuple-element.272, f32[8,1024,1024]{1,2,0:T(8,128)} %fusion.111, f32[8,1024]{1,0:T(8,128)S(1)} %get-tuple-element.273, f32[8,1024]{1,0:T(8,128)S(1)} %dynamic-slice_bitcast_fusion.8, ...), kind=kLoop, calls=%fused_computation.16.clone.1 | loop fusion | flops 58720256 | bytes 100859904 | tf_op jit(solution)/shard_map/while/body/eval_jaxpr/convert_element_type | solution.py:81
  896.8 35.2 %psum.77 = bf16[2048]{0:T(1024)(128)(2,1)S(1)} all-reduce(bf16[2048]{0:T(1024)(128)(2,1)S(1)} %copy-done.40), channel_id=1, replica_groups=mesh['dp'=16,'mp'=2] {'dp'}, use_global_device_ids=true, to_apply=%region_32.33 | all-reduce | flops 2048 | bytes 8192 | tf_op jit(solution)/shard_map/psum | solution.py:199
  932.7 186.7 %all-reduce.4.cloned.1.call-done = (bf16[1024,1536]{1,0:T(8,128)(2,1)}, bf16[512,1024]{1,0:T(8,128)(2,1)}, bf16[1024,2048]{1,0:T(8,128)(2,1)}, bf16[2048,1024]{1,0:T(8,128)(2,1)}) async-done(((bf16[1024,1536]{1,0:T(8,128)(2,1)}, bf16[512,1024]{1,0:T(8,128)(2,1)}, bf16[1024,2048]{1,0:T(8,128)(2,1)}, bf16[2048,1024]{1,0:T(8,128)(2,1)}), (bf16[1024,1536]{1,0:T(8,128)(2,1)}, bf16[512,1024]{1,0:T(8,128)(2,1)}, ...) | async-done | bytes 12582928 | tf_op jit(solution)/shard_map/psum | solution.py:196
  1136.5 40.2 %reduce-scatter.11.cloned.1.call-done = bf16[1024,1024]{1,0:T(8,128)(2,1)} async-done(((bf16[2048,1024]{1,0:T(8,128)(2,1)}), bf16[1024,1024]{1,0:T(8,128)(2,1)}) %reduce-scatter.11.cloned.1.call-update) | async-done | bytes 2097168 | tf_op jit(solution)/shard_map/reduce_scatter | solution.py:184
  1187.5 39.8 %all-reduce = (f32[1024]{0:T(1024)}, f32[1024]{0:T(1024)}, f32[1024]{0:T(1024)}, f32[1024]{0:T(1024)}, f32[1024]{0:T(1024)}) all-reduce(f32[1024]{0:T(1024)S(1)} %get-tuple-element.140, f32[1024]{0:T(1024)S(1)} %get-tuple-element.143, f32[1024]{0:T(1024)S(1)} %copy-done.36, ...), channel_id=1, replica_groups=mesh['dp'=16,'mp'=2] {'dp','mp'}, use_global_device_ids=true, to_apply=%region_21.22 | all-reduce | flops 5120 | bytes 40960 | tf_op jit(solution)/shard_map/psum | solution.py:202
  (194 shorter events, 358.5 us)
Async XLA Ops:
  7.2 228.5 %copy-start = (bf16[512,1024]{1,0:T(8,128)(2,1)S(1)}, bf16[512,1024]{1,0:T(8,128)(2,1)}, u32[]{:S(2)}) copy-start(bf16[512,1024]{1,0:T(8,128)(2,1)} %param.26) | copy-start | bytes 3145732
  7.2 67.4 %all-gather.4.cloned.1.call-start = ((), (), s32[]{:S(2)}) async-start(), calls=%async_computation.4 | async-start | bytes 6291456 | tf_op jit(solution)/shard_map/all_gather | solution.py:119
  15.1 279.5 %reduce-scatter.5.cloned.1.call-start = ((), (), s32[]{:S(2)}) async-start(), calls=%async_computation.5 | async-start | bytes 6291456 | tf_op jit(solution)/shard_map/reduce_scatter | solution.py:126
  240.0 54.5 %copy-start.5 = (bf16[1024,1024]{1,0:T(8,128)(2,1)S(1)}, bf16[1024,1024]{1,0:T(8,128)(2,1)}, u32[]{:S(2)}) copy-start(bf16[1024,1024]{1,0:T(8,128)(2,1)} %param.19) | copy-start | bytes 6291460
  240.1 57.8 %copy-start.35 = (f32[1024]{0:T(1024)S(1)}, f32[1024]{0:T(1024)}, u32[]{:S(2)}) copy-start(f32[1024]{0:T(1024)} %param.27) | copy-start | bytes 12292
  240.1 57.8 %copy-start.39 = (f32[1024]{0:T(1024)S(1)}, f32[1024]{0:T(1024)}, u32[]{:S(2)}) copy-start(f32[1024]{0:T(1024)} %param.28) | copy-start | bytes 12292
  240.1 168.5 %all-gather.6.cloned.1.call-start = ((), (), s32[]{:S(2)}) async-start(), calls=%async_computation.7 | async-start | bytes 6291456 | tf_op jit(solution)/shard_map/all_gather | solution.py:150
  300.2 83.1 %collective-permute-start = (bf16[1024,1024]{1,0:T(8,128)(2,1)}, bf16[1024,1024]{1,0:T(8,128)(2,1)}, u32[]{:S(2)}, u32[]{:S(2)}) collective-permute-start(bf16[1024,1024]{1,0:T(8,128)(2,1)} %add_convert_fusion.1), channel_id=1, source_target_pairs={{0,1},{1,0},{2,3},{3,2},{4,5},{5,4},{6,7},{7,6},{8,9},{9,8},{10,11... | collective-permute-start | bytes 6291464 | tf_op jit(solution)/shard_map/ppermute | solution.py:16
  300.6 203.5 %reduce-scatter.9.cloned.1.call-start = ((), (), s32[]{:S(2)}) async-start(), calls=%async_computation.8 | async-start | bytes 6291456 | tf_op jit(solution)/shard_map/reduce_scatter | solution.py:157
  300.6 91.5 %copy-start.43 = (bf16[1024,2048]{1,0:T(8,128)(2,1)S(1)}, bf16[1024,2048]{1,0:T(8,128)(2,1)}, u32[]{:S(2)}) copy-start(bf16[1024,2048]{1,0:T(8,128)(2,1)} %param.29) | copy-start | bytes 12582916
  300.6 91.5 %copy-start.46 = (f32[2048]{0:T(1024)S(1)}, f32[2048]{0:T(1024)}, u32[]{:S(2)}) copy-start(f32[2048]{0:T(1024)} %param.30) | copy-start | bytes 24580
  408.6 28.0 %copy-start.44 = (bf16[1024,2048]{1,0:T(8,128)(2,1)S(1)}, bf16[1024,2048]{1,0:T(8,128)(2,1)}, u32[]{:S(2)}) copy-start(bf16[1024,2048]{1,0:T(8,128)(2,1)} %param.29) | copy-start | bytes 12582916
  449.6 110.9 %reduce-scatter.7.cloned.1.call-start = ((), (), s32[]{:S(2)}) async-start(), calls=%async_computation.6 | async-start | bytes 6291456 | tf_op jit(solution)/shard_map/reduce_scatter | solution.py:139
  463.5 97.0 %copy-start.42 = (f32[1024]{0:T(1024)S(1)}, f32[1024]{0:T(1024)}, u32[]{:S(2)}) copy-start(f32[1024]{0:T(1024)} %param.32) | copy-start | bytes 12292
  463.5 163.4 %all-gather.8.cloned.1.call-start = ((), (), s32[]{:S(2)}) async-start(), calls=%async_computation.9 | async-start | bytes 6291456 | tf_op jit(solution)/shard_map/all_gather | solution.py:169
  569.9 549.4 %all-reduce.4.cloned.1.call-start = ((), (), s32[]{:S(2)}) async-start(), calls=%async_computation.11 | async-start | bytes 25165824 | tf_op jit(solution)/shard_map/psum | solution.py:196
  884.2 292.4 %reduce-scatter.11.cloned.1.call-start = ((), (), s32[]{:S(2)}) async-start(), calls=%async_computation.10 | async-start | bytes 6291456 | tf_op jit(solution)/shard_map/reduce_scatter | solution.py:184
  1133.4 43.2 %copy-start.6 = (bf16[1024,1024]{1,0:T(8,128)(2,1)S(1)}, bf16[1024,1024]{1,0:T(8,128)(2,1)}, u32[]{:S(2)}) copy-start(bf16[1024,1024]{1,0:T(8,128)(2,1)} %param.19) | copy-start | bytes 6291460
  1133.4 43.2 %copy-start.26 = (f32[1024]{0:T(1024)S(1)}, f32[1024]{0:T(1024)}, u32[]{:S(2)}) copy-start(f32[1024]{0:T(1024)} %copy-done.25) | copy-start | bytes 12292
  1133.4 43.2 %copy-start.30 = (f32[1024]{0:T(1024)S(1)}, f32[1024]{0:T(1024)}, u32[]{:S(2)}) copy-start(f32[1024]{0:T(1024)} %param.21) | copy-start | bytes 12292
  1136.4 43.3 %copy-start.34 = (f32[1024]{0:T(1024)S(1)}, f32[1024]{0:T(1024)}, u32[]{:S(2)}) copy-start(f32[1024]{0:T(1024)} %copy-done.33) | copy-start | bytes 12292
  1136.4 43.3 %copy-start.28 = (f32[1024]{0:T(1024)S(1)}, f32[1024]{0:T(1024)}, u32[]{:S(2)}) copy-start(f32[1024]{0:T(1024)} %copy-done.27) | copy-start | bytes 12292
  1136.5 47.3 %copy-start.32 = (f32[1024]{0:T(1024)S(1)}, f32[1024]{0:T(1024)}, u32[]{:S(2)}) copy-start(f32[1024]{0:T(1024)} %copy-done.31) | copy-start | bytes 12292
  1183.7 43.6 %copy-start.1 = (bf16[512,1024]{1,0:T(8,128)(2,1)S(1)}, bf16[512,1024]{1,0:T(8,128)(2,1)}, u32[]{:S(2)}) copy-start(bf16[512,1024]{1,0:T(8,128)(2,1)} %param.26) | copy-start | bytes 3145732
  (34 other events, 208.2 us)
Sparse Core Ops, SparseCore 0:
  15.2 59.4 all-gather.3
  240.2 54.3 reduce-scatter.4
  300.7 92.2 all-gather.5
  449.7 54.2 reduce-scatter.8
  506.2 54.3 reduce-scatter.6
  570.1 56.7 all-gather.7
  884.3 234.9 all-reduce.3
  1122.3 54.3 reduce-scatter.10
